TPU v7x, 768 devices: a whole 4x8x12 slice. The times are simulated.
768 devices in a mesh: pts: 96 (over x, y, z_hi), cells: 8 (over z_lo, core).
Axes of the slice: x: 4, y: 8, z: 12 (z_hi: 3, z_lo: 4; z = z_hi * 4 + z_lo), core: 2. Of those that a mesh axis runs over, the one named last changes fastest.
Arguments:
- codes: int32 [49152, 512], P(('pts', 'cells')), may hold values from -127 to 127
- exponents: int32 [49152], P(('pts', 'cells')), may hold values from 6 to 9
- centroids: bfloat16 [24576, 512], P('cells'), as said below
- counters: int32 [24576], P('cells'), may hold values from 0 to 4095
Outputs:
- cell_sums: float32 [8, 3072, 512], P('cells', 'pts')
- cell_mass: float32 [8, 3072], P('cells', 'pts')
Inputs may be any that keep to these rules, and one draw needn't show every extreme that they name: `centroids`: centroids are real-valued with row scales that differ from row to row.
All inputs are finite; a program needn't handle non-finite values.
Results may differ from a plain program's by a relative error of at most 0.013.
Values may be sent and summed in bfloat16 or wider, within the bound.
A program may use at most 32 MiB of HBM per device.

v0:
```python
import math

import jax
import jax.numpy as jnp
from jax import lax
from jax.sharding import PartitionSpec as P


def body(codes, exponents, centroids, counters):
    scaled = codes.astype(jnp.float32) * jnp.exp2(-exponents.astype(jnp.float32))[:, None]
    local_rows = scaled.astype(jnp.bfloat16)
    points = lax.all_gather(local_rows, "cells", axis=0, tiled=True)
    width = points.shape[1]
    beta = 4.0 / math.sqrt(width)
    logits = (
        lax.dot_general(
            points, centroids, (((1,), (1,)), ((), ())), preferred_element_type=jnp.float32
        )
        * beta
    )
    inverse = lax.rsqrt(counters.astype(jnp.float32) + 1.0)
    local_top = jnp.max(logits, axis=1)
    top = lax.pmax(local_top, "cells")
    expo = jnp.exp(logits - top[:, None])
    total, novel = lax.psum(
        (jnp.sum(expo, axis=1), jnp.dot(expo, inverse, preferred_element_type=jnp.float32)), "cells"
    )
    weight = novel / total
    share = (expo * (weight / total)[:, None]).astype(jnp.bfloat16)
    mass_local = jnp.sum(share.astype(jnp.float32), axis=0)
    sums_local = lax.dot_general(
        share, points, (((0,), (0,)), ((), ())), preferred_element_type=jnp.float32
    )
    sums, mass = (
        lax.psum_scatter(sums_local, "pts", scatter_dimension=0, tiled=True),
        lax.psum_scatter(mass_local, "pts", scatter_dimension=0, tiled=True),
    )
    return (sums[None], mass[None])


def solution(mesh):
    in_specs = (P(("pts", "cells"), None), P(("pts", "cells")), P("cells", None), P("cells"))
    out_specs = (P("cells", "pts", None), P("cells", "pts"))
    return jax.shard_map(body, mesh=mesh, in_specs=in_specs, out_specs=out_specs, check_vma=False)
```

profile of v0, /device:TPU:128, one launch (start us, length us, event | category | flops | bytes accessed | tf_op | source)
XLA Modules:
  0.0 765.6 jit_solution(11995461397053791679)
XLA Ops:
  7.2 0.0 copy-start
  7.2 0.0 copy-start.4
  7.2 0.0 reduce-scatter.2.cloned.1.call-start
  7.2 0.8 multiply_exponential_fusion
  8.0 1.1 multiply_convert_fusion.1
  9.1 20.5 %all_gather.3 = bf16[512,512]{1,0:T(8,128)(2,1)S(1)} all-gather(bf16[64,512]{1,0:T(8,128)(2,1)S(1)} %multiply_convert_fusion.1), channel_id=1, replica_groups=mesh['pts'=96,'cells'=8] {'cells'}, dimensions={0}, use_global_device_ids=true | all-gather | bytes 589824 | tf_op jit(solution)/shard_map/all_gather | solution.py:12
  29.6 0.0 copy-start.2
  29.6 0.8 copy-done.2
  30.4 0.0 copy-done
  30.4 4.5 multiply_reduce_fusion
  34.9 10.5 %pmax.7 = f32[512]{0:T(512)S(1)} all-reduce(f32[512]{0:T(512)S(1)} %get-tuple-element.6), channel_id=1, replica_groups=mesh['pts'=96,'cells'=8] {'cells'}, use_global_device_ids=true, to_apply=%region_1.0 | all-reduce | flops 512 | bytes 4096 | tf_op jit(solution)/shard_map/pmax | solution.py:23
  45.4 0.0 copy-done.4
  45.5 0.0 copy-start.1
  45.5 4.1 fusion
  49.6 0.5 copy-done.1
  50.1 1.1 fusion.1
  51.2 13.1 %all-reduce.1 = (f32[512]{0:T(512)S(1)}, f32[512]{0:T(512)S(1)}) all-reduce(f32[512]{0:T(512)S(1)} %bitcast.12, f32[512]{0:T(512)S(1)} %fusion), channel_id=1, replica_groups=mesh['pts'=96,'cells'=8] {'cells'}, use_global_device_ids=true, to_apply=%region_2.0 | all-reduce | flops 1024 | bytes 8192 | tf_op jit(solution)/shard_map/psum | solution.py:25
  64.3 0.0 copy-start.3
  64.3 3.8 convert_reduce_fusion
  68.1 0.0 copy-done.3
  68.1 4.5 fusion.5
  72.6 0.0 reduce-scatter.2.cloned.1.call-update
  72.7 1.3 dynamic-slice
  74.6 658.0 %all-reduce = f32[3072]{0:T(1024)S(1)} all-reduce(f32[3072]{0:T(1024)S(1)} %get-tuple-element.4), channel_id=3, replica_groups=mesh['pts'=96,'cells'=8] {'pts'}, use_global_device_ids=true, to_apply=%region_7.0.clone | all-reduce | flops 3072 | bytes 24576
  732.6 0.6 dynamic-slice_bitcast_fusion
  733.2 25.6 %reduce-scatter.2.cloned.1.call-done = f32[32,512]{1,0:T(8,128)} async-done(((f32[3072,512]{1,0:T(8,128)}), f32[32,512]{1,0:T(8,128)}) %reduce-scatter.2.cloned.1.call-update) | async-done | bytes 65552 | tf_op jit(solution)/shard_map/reduce_scatter | solution.py:35
  (2 shorter events, 0.0 us)
Async XLA Ops:
  7.2 23.3 %copy-start = (bf16[3072,512]{1,0:T(8,128)(2,1)S(1)}, bf16[3072,512]{1,0:T(8,128)(2,1)}, u32[]{:S(2)}) copy-start(bf16[3072,512]{1,0:T(8,128)(2,1)} %param.6) | copy-start | bytes 9437188
  7.2 38.3 %copy-start.4 = (s32[3072]{0:T(1024)S(1)}, s32[3072]{0:T(1024)}, u32[]{:S(2)}) copy-start(s32[3072]{0:T(1024)} %param.7) | copy-start | bytes 36868
  7.2 751.6 %reduce-scatter.2.cloned.1.call-start = ((), (), s32[]{:S(2)}) async-start(), calls=%async_computation.1 | async-start | bytes 6356992 | tf_op jit(solution)/shard_map/reduce_scatter | solution.py:35
  29.6 0.8 copy-start.2
  45.5 4.6 copy-start.1
  64.3 3.8 copy-start.3
Sparse Core Ops, SparseCore 0:
  72.8 685.9 reduce-scatter.1
where the time goes:
time: 766 us
  blocking collectives  702 us (92%)
  waiting for transfers between devices  25.6 us (3%)
  between operations  14.7 us (2%)
  matrix products  10.2 us (1%)
  other arithmetic  9.76 us (1%)
    unnamed x1, blocking collectives  658 us
    reduce_scatter x1, waiting for transfers between devices, body(): lax.psum_scatter(sums_local, 'pts', scatter_dimension=0, tiled=True)  25.6 us
    all_gather x1, blocking collectives, body(): points = lax.all_gather(local_rows, 'cells', axis=0, tiled=True)  20.5 us
  transfers between devices with their start and end apart: 1, of which 1 were waited for; matrix products, arithmetic and copies ran while one was open for 0% of the time, Pallas kernels for 0%

commit v1 on v0

v1 whole, which is shorter than its diff:
```python
import functools
import math

import jax
import jax.numpy as jnp
from jax import lax
from jax.experimental import pallas as pl
from jax.experimental.pallas import tpu as pltpu
from jax.sharding import PartitionSpec as P

X, Y, ZH, ZL, CORES = 4, 8, 3, 4, 2
MESH = pl.DeviceIdType.MESH
F32, BF16 = jnp.float32, jnp.bfloat16


def power_of_minus(e):
    value = jnp.ones(e.shape, F32)
    for bit in range(7):
        step = jnp.full(e.shape, 2.0 ** -(2**bit), F32)
        value = value * jnp.where(((e >> bit) & 1) == 1, step, 1.0)
    return value


def dot_nt(a, b):
    return lax.dot_general(a, b, (((1,), (1,)), ((), ())), preferred_element_type=F32)


def kernel(
    scale,
    codes_hbm, exps_ref, cent_hbm, counters_ref,
    sums_ref, mass_ref,
    codes, cent, pts, inv, tmp, logit, share, acc, massacc,
    stats, rm, y_out, y_in, m_out, my_in, z_out, z_in, mz_out, mz_in,
    load_sem, g_send, g_recv, s_send, s_recv, r_send, r_recv,
    y_send, y_recv, my_send, my_recv, z_send, z_recv, mz_send, mz_recv,
):
    p = lax.axis_index("pts")
    me = lax.axis_index("cells")
    x = lax.div(p, Y * ZH)
    y = lax.rem(lax.div(p, ZH), Y)
    zh = lax.rem(p, ZH)
    zl = lax.div(me, CORES)
    core = lax.rem(me, CORES)
    other = 1 - core
    peers = ZL * CORES
    rows, width = pts.shape[3:]
    chunk = CORES * rows
    slice_rows = cent.shape[1]
    y_rows, z_rows = y_in.shape[1], z_in.shape[1]

    def at_x(j):
        xx = lax.rem(x + j, X)
        return ((xx * Y + y) * ZH + zh, me)

    def at_y(k):
        yy = lax.rem(y + k, Y)
        return ((x * Y + yy) * ZH + zh, me)

    def at_z(k):
        return ((x * Y + y) * ZH + lax.rem(zh + k, ZH), me)

    sibling = (p, zl * CORES + other)

    load_codes = pltpu.make_async_copy(codes_hbm, codes, load_sem.at[0])
    load_cent = pltpu.make_async_copy(cent_hbm, cent, load_sem.at[1])
    load_codes.start()
    load_cent.start()

    barrier = pltpu.get_barrier_semaphore()

    def greet(device):
        pl.semaphore_signal(barrier, inc=1, device_id=device, device_id_type=MESH)

    for k in range(1, Y):
        greet(at_y(k))
    for k in range(1, ZH):
        greet(at_z(k))
    for k in range(1, peers):
        greet((p, lax.rem(me + k, peers)))
    for j in range(1, X):
        greet(at_x(j))

    n_exp = exps_ref.shape[1]
    powers = power_of_minus(exps_ref[...])
    diagonal = lax.broadcasted_iota(jnp.int32, (n_exp, n_exp), 0) == lax.broadcasted_iota(
        jnp.int32, (n_exp, n_exp), 1
    )
    column = jnp.sum(jnp.where(diagonal, powers, 0.0), axis=1, keepdims=True)
    load_codes.wait()
    pts[x, zl, core] = (codes[...].astype(F32) * column).astype(BF16)

    pl.semaphore_wait(barrier, (Y - 1) + (ZH - 1) + (peers - 1) + (X - 1))

    def block(xx, zz, cc, device, sem):
        return pltpu.make_async_remote_copy(
            src_ref=pts.at[xx, zz, cc], dst_ref=pts.at[xx, zz, cc],
            send_sem=g_send.at[sem], recv_sem=g_recv.at[xx, zz, cc],
            device_id=device, device_id_type=MESH,
        )

    block(x, zl, core, sibling, 0).start()
    for k in range(1, ZL):
        block(x, zl, core, (p, lax.rem(zl + k, ZL) * CORES + core), k).start()
    for j in range(1, X):
        block(x, zl, core, at_x(j), ZL - 1 + j).start()
    sem_zl = ZL + X - 1

    square = (128, 128)
    eye = lax.broadcasted_iota(jnp.int32, square, 0) == lax.broadcasted_iota(jnp.int32, square, 1)

    def spread(g, carry):
        row = lax.rsqrt(counters_ref[pl.ds(g, 1), :].astype(F32) + 1.0)
        col = jnp.sum(jnp.where(eye, row, 0.0), axis=1, keepdims=True)
        inv[pl.ds(pl.multiple_of(g * 128, 128), 128), :] = jnp.broadcast_to(col, square)
        return carry

    lax.fori_loop(0, counters_ref.shape[0], spread, 0)
    load_cent.wait()

    def stat_copy(src, zz, k):
        return pltpu.make_async_remote_copy(
            src_ref=stats.at[src, zz], dst_ref=stats.at[src, zz],
            send_sem=s_send.at[k, zz], recv_sem=s_recv.at[src, zz],
            device_id=(p, lax.rem(me + k, peers)), device_id_type=MESH,
        )

    def local_stats(zz):
        points = pts[x, zz].reshape(chunk, width)

        def product(s, top):
            part = dot_nt(cent[s], points)
            tmp[s] = part
            return jnp.maximum(top, jnp.max(part, axis=0, keepdims=True))

        top = lax.fori_loop(0, X, product, jnp.full((1, chunk), -jnp.inf, F32))
        shift = top * scale

        def add_up(s, sums):
            expo = jnp.exp2(tmp[s] * scale - shift)
            weights = inv[pl.ds(pl.multiple_of(s * slice_rows, 128), slice_rows), :]
            return (
                sums[0] + jnp.sum(expo, axis=0, keepdims=True),
                sums[1] + jnp.sum(expo * weights, axis=0, keepdims=True),
            )

        zero = jnp.zeros((1, chunk), F32)
        total, novel = lax.fori_loop(0, X, add_up, (zero, zero))
        logit[x, :, pl.ds(pl.multiple_of(zz * chunk, 128), chunk)] = tmp[x]
        stats[me, zz, 0:1, :] = top
        stats[me, zz, 1:2, :] = total
        stats[me, zz, 2:3, :] = novel

        def send(k, carry):
            stat_copy(me, zz, k).start()
            return carry

        lax.fori_loop(1, peers, send, 0)

    block(x, zl, other, sibling, 0).wait_recv()
    local_stats(zl)
    if ZL == 4:
        first = zl + 1 - 2 * lax.div(zl, 2)
        last = 3 - 3 * lax.div(zl, 2)
        order = [first, 6 - zl - first - last, last]
    else:
        order = [lax.rem(zl + k, ZL) for k in range(1, ZL)]
    for k, zz in enumerate(order):
        block(x, zz, core, sibling, 0).wait_recv()
        for j in range(1, X):
            block(x, zz, core, at_x(j), sem_zl + k * X + j).start()
        block(x, zz, core, sibling, sem_zl + k * X).start()
        block(x, zz, other, sibling, 0).wait_recv()
        local_stats(zz)
    sem_x = sem_zl + (ZL - 1) * X

    x_order = [1, 3, 2] if X == 4 else list(range(1, X))
    for i, j in enumerate(x_order):
        xx = lax.rem(x + j, X)

        def pass_on(zz, carry, i=i, xx=xx):
            block(xx, zz, core, sibling, 0).wait_recv()
            block(xx, zz, core, sibling, sem_x + i * ZL + zz).start()
            return carry

        lax.fori_loop(0, ZL, pass_on, 0)
    for j in x_order:
        xx = lax.rem(x + j, X)

        def arrived(zz, carry, xx=xx):
            block(xx, zz, other, sibling, 0).wait_recv()
            return carry

        lax.fori_loop(0, ZL, arrived, 0)
        logit[xx] = dot_nt(cent[x], pts[xx].reshape(ZL * chunk, width))

    def stats_in(k, carry):
        src = lax.rem(me + k, peers)

        def one(zz, inner):
            stat_copy(src, zz, k).wait_recv()
            return inner

        return lax.fori_loop(0, ZL, one, carry)

    lax.fori_loop(1, peers, stats_in, 0)

    def combine(zz, carry):
        tops = stats[:, zz, 0, :]
        top = jnp.max(tops, axis=0, keepdims=True)
        ratio = jnp.exp2((tops - top) * scale)
        total = jnp.sum(stats[:, zz, 1, :] * ratio, axis=0, keepdims=True)
        novel = jnp.sum(stats[:, zz, 2, :] * ratio, axis=0, keepdims=True)
        rm[x, zz, 0:1, :] = top * scale
        rm[x, zz, 1:2, :] = novel / total / total
        return carry

    lax.fori_loop(0, ZL, combine, 0)

    def rm_copy(src, j):
        return pltpu.make_async_remote_copy(
            src_ref=rm.at[src], dst_ref=rm.at[src],
            send_sem=r_send.at[j], recv_sem=r_recv.at[src],
            device_id=at_x(j), device_id_type=MESH,
        )

    for j in range(1, X):
        rm_copy(x, j).start()

    acc[...] = jnp.zeros(acc.shape, F32)
    massacc[...] = jnp.zeros(massacc.shape, F32)

    def accumulate(xx):
        for zz in range(ZL):
            lanes = slice(zz * chunk, (zz + 1) * chunk)
            shift, factor = rm[xx, zz, 0:1, :], rm[xx, zz, 1:2, :]
            part = (jnp.exp2(logit[xx, :, lanes] * scale - shift) * factor).astype(BF16)
            share[:, lanes] = part
            massacc[...] += part.astype(F32)
        acc[...] += jnp.dot(
            share[...], pts[xx].reshape(ZL * chunk, width), preferred_element_type=F32
        )

    accumulate(x)
    for j in x_order:
        xx = lax.rem(x + j, X)
        rm_copy(xx, j).wait_recv()
        accumulate(xx)

    def y_copy(src, k, dst):
        return pltpu.make_async_remote_copy(
            src_ref=y_out.at[dst], dst_ref=y_in.at[src],
            send_sem=y_send.at[k], recv_sem=y_recv.at[src],
            device_id=at_y(k), device_id_type=MESH,
        )

    def my_copy(src, k):
        return pltpu.make_async_remote_copy(
            src_ref=m_out, dst_ref=my_in.at[src],
            send_sem=my_send.at[k], recv_sem=my_recv.at[src],
            device_id=at_y(k), device_id_type=MESH,
        )

    def y_start(k, carry):
        dst = lax.rem(y + k, Y)
        y_out[dst] = acc[pl.ds(pl.multiple_of(dst * y_rows, 16), y_rows), :].astype(BF16)
        y_copy(y, k, dst).start()
        return carry

    lax.fori_loop(1, Y, y_start, 0)

    m_out[...] = jnp.zeros(m_out.shape, F32)
    for g in range(slice_rows // 128):
        col = jnp.sum(massacc[g * 128 : (g + 1) * 128, :], axis=1, keepdims=True)
        m_out[g : g + 1, :] = jnp.sum(jnp.where(eye, col, 0.0), axis=0, keepdims=True)

    def my_start(k, carry):
        my_copy(y, k).start()
        return carry

    lax.fori_loop(1, Y, my_start, 0)

    own = pl.ds(pl.multiple_of(y * y_rows, 16), y_rows)

    def y_add(k, total):
        src = lax.rem(y + k, Y)
        y_copy(src, k, src).wait_recv()
        acc[own, :] += y_in[src].astype(F32)
        my_copy(src, k).wait_recv()
        return total + my_in[src]

    mass = lax.fori_loop(1, Y, y_add, m_out[...])

    def z_copy(src, k, dst):
        return pltpu.make_async_remote_copy(
            src_ref=z_out.at[dst], dst_ref=z_in.at[src],
            send_sem=z_send.at[k], recv_sem=z_recv.at[src],
            device_id=at_z(k), device_id_type=MESH,
        )

    def mz_copy(src, k):
        return pltpu.make_async_remote_copy(
            src_ref=mz_out, dst_ref=mz_in.at[src],
            send_sem=mz_send.at[k], recv_sem=mz_recv.at[src],
            device_id=at_z(k), device_id_type=MESH,
        )

    mz_out[...] = mass
    for k in range(1, ZH):
        dst = lax.rem(zh + k, ZH)
        begin = y * y_rows + dst * z_rows
        z_out[dst] = acc[pl.ds(pl.multiple_of(begin, 16), z_rows), :].astype(BF16)
        z_copy(zh, k, dst).start()
        mz_copy(zh, k).start()
    begin = y * y_rows + zh * z_rows
    result = acc[pl.ds(pl.multiple_of(begin, 16), z_rows), :]
    for k in range(1, ZH):
        src = lax.rem(zh + k, ZH)
        z_copy(src, k, src).wait_recv()
        mz_copy(src, k).wait_recv()
        result = result + z_in[src].astype(F32)
        mass = mass + mz_in[src]
    sums_ref[...] = result

    per_row = 128 // z_rows
    place = y * ZH + zh
    line = lax.div(place, per_row)
    which = lax.rem(place, per_row)
    at_line = lax.broadcasted_iota(jnp.int32, mass.shape, 0) == line
    picked = jnp.sum(jnp.where(at_line, mass, 0.0), axis=0, keepdims=True)
    answer = jnp.zeros((1, z_rows), F32)
    for q in range(per_row):
        answer = jnp.where(which == q, picked[:, q * z_rows : (q + 1) * z_rows], answer)
    mass_ref[...] = answer

    def sent_block(i, carry):
        block(x, zl, core, sibling, i).wait_send()
        return carry

    lax.fori_loop(0, g_send.shape[0], sent_block, 0)

    def sent_stats(k, carry):
        def one(zz, inner):
            stat_copy(me, zz, k).wait_send()
            return inner

        return lax.fori_loop(0, ZL, one, carry)

    lax.fori_loop(1, peers, sent_stats, 0)
    for j in range(1, X):
        rm_copy(x, j).wait_send()

    def sent_y(k, carry):
        y_copy(y, k, lax.rem(y + k, Y)).wait_send()
        my_copy(y, k).wait_send()
        return carry

    lax.fori_loop(1, Y, sent_y, 0)
    for k in range(1, ZH):
        z_copy(zh, k, lax.rem(zh + k, ZH)).wait_send()
        mz_copy(zh, k).wait_send()


def body(codes, exponents, centroids, counters):
    rows, width = codes.shape
    cells = centroids.shape[0]
    slice_rows = cells // X
    y_rows = slice_rows // Y
    z_rows = y_rows // ZH
    chunk = CORES * rows
    line = ZL * chunk
    peers = ZL * CORES
    scale = 4.0 / math.sqrt(width) * math.log2(math.e)
    vmem, dma = pltpu.VMEM, pltpu.SemaphoreType.DMA
    sums, mass = pl.pallas_call(
        functools.partial(kernel, scale),
        out_shape=(
            jax.ShapeDtypeStruct((z_rows, width), F32),
            jax.ShapeDtypeStruct((1, z_rows), F32),
        ),
        in_specs=[
            pl.BlockSpec(memory_space=pl.ANY),
            pl.BlockSpec(memory_space=vmem),
            pl.BlockSpec(memory_space=pl.ANY),
            pl.BlockSpec(memory_space=vmem),
        ],
        out_specs=(pl.BlockSpec(memory_space=vmem), pl.BlockSpec(memory_space=vmem)),
        scratch_shapes=[
            vmem((rows, width), jnp.int32),
            vmem((X, slice_rows, width), BF16),
            vmem((X, ZL, CORES, rows, width), BF16),
            vmem((cells, 128), F32),
            vmem((X, slice_rows, chunk), F32),
            vmem((X, slice_rows, line), F32),
            vmem((slice_rows, line), BF16),
            vmem((slice_rows, width), F32),
            vmem((slice_rows, chunk), F32),
            vmem((peers, ZL, 8, chunk), F32),
            vmem((X, ZL, 8, chunk), F32),
            vmem((Y, y_rows, width), BF16),
            vmem((Y, y_rows, width), BF16),
            vmem((8, 128), F32),
            vmem((Y, 8, 128), F32),
            vmem((ZH, z_rows, width), BF16),
            vmem((ZH, z_rows, width), BF16),
            vmem((8, 128), F32),
            vmem((ZH, 8, 128), F32),
            dma((2,)),
            dma((X + ZL - 1 + (ZL - 1) * X + (X - 1) * ZL,)),
            dma((X, ZL, CORES)),
            dma((peers, ZL)),
            dma((peers, ZL)),
            dma((X,)),
            dma((X,)),
            dma((Y,)),
            dma((Y,)),
            dma((Y,)),
            dma((Y,)),
            dma((ZH,)),
            dma((ZH,)),
            dma((ZH,)),
            dma((ZH,)),
        ],
        compiler_params=pltpu.CompilerParams(
            collective_id=0, has_side_effects=True, vmem_limit_bytes=48 << 20
        ),
    )(
        codes,
        exponents.reshape(1, rows),
        centroids.reshape(X, slice_rows, width),
        counters.reshape(cells // 128, 128),
    )
    return sums[None], mass


def solution(mesh):
    in_specs = (P(("pts", "cells"), None), P(("pts", "cells")), P("cells", None), P("cells"))
    out_specs = (P("cells", "pts", None), P("cells", "pts"))
    return jax.shard_map(body, mesh=mesh, in_specs=in_specs, out_specs=out_specs, check_vma=False)
```

time: 766 us -> 78 us (0.10)
  the two profiles are of different devices: /device:TPU:128 before, /device:TPU:1 now
where the time goes in v1:
time: 78 us; the launch traced here: 76.8 us
  Pallas kernels  70.9 us (91%)
  local copies, waits for them, and re-layouts  5.29 us (7%)
    pallas_call x1, Pallas kernels, body(): pl.pallas_call(functools.partial(kernel, scale), out_shape=(jax.ShapeDtyp...  70.9 us
    unnamed x10, local copies, waits for them, and re-layouts  5.29 us

profile of v1, /device:TPU:1, one launch (start us, length us, event | category | flops | bytes accessed | tf_op | source)
XLA Modules:
  0.0 76.8 jit_solution(14206095498954557176)
XLA Ops:
  0.6 0.0 copy-start
  0.6 1.9 %copy-done = bf16[3072,512]{1,0:T(8,128)(2,1)S(1)} copy-done((bf16[3072,512]{1,0:T(8,128)(2,1)S(1)}, bf16[3072,512]{1,0:T(8,128)(2,1)}, u32[]{:S(2)}) %copy-start) | copy-done | bytes 3145752
  2.5 0.0 copy-start.1
  2.5 0.9 %copy-done.1 = s32[64,512]{1,0:T(8,128)S(1)} copy-done((s32[64,512]{1,0:T(8,128)S(1)}, s32[64,512]{1,0:T(8,128)}, u32[]{:S(2)}) %copy-start.1) | copy-done | bytes 131096
  3.4 0.0 copy-start.2
  3.4 0.7 copy-done.2
  4.1 0.0 copy-start.3
  4.1 0.7 copy-done.3
  4.8 70.9 %shard_map.59 = (f32[32,512]{1,0:T(8,128)S(1)}, f32[1,32]{1,0:T(1,128)S(1)}) custom-call(s32[64,512]{1,0:T(8,128)S(1)} %copy-done.1, s32[1,64]{1,0:T(1,128)S(1)} %bitcast.7, bf16[4,768,512]{2,1,0:T(8,128)(2,1)S(1)} %bitcast.4, s32[24,128]{1,0:T(8,128)S(1)} %bitcast.6), custom_call_target="tpu_custom_call" | custom-call | tf_op jit(solution)/shard_map/pallas_call | solution.py:374
  75.7 0.6 copy.8
  76.3 0.5 copy.9
Async XLA Ops:
  0.6 1.9 %copy-start = (bf16[3072,512]{1,0:T(8,128)(2,1)S(1)}, bf16[3072,512]{1,0:T(8,128)(2,1)}, u32[]{:S(2)}) copy-start(bf16[3072,512]{1,0:T(8,128)(2,1)} %param.6) | copy-start | bytes 9437188
  2.5 0.9 %copy-start.1 = (s32[64,512]{1,0:T(8,128)S(1)}, s32[64,512]{1,0:T(8,128)}, u32[]{:S(2)}) copy-start(s32[64,512]{1,0:T(8,128)} %codes_hbm.1) | copy-start | bytes 393220
  3.4 0.7 copy-start.2
  4.1 0.7 copy-start.3

commit v2 on v1

v2 whole, which is shorter than its diff:
```python
import functools
import math

import jax
import jax.numpy as jnp
from jax import lax
from jax.experimental import pallas as pl
from jax.experimental.pallas import tpu as pltpu
from jax.sharding import PartitionSpec as P

X, Y, ZH, ZL, CORES = 4, 8, 3, 4, 2
NY, NZ = 2, 2
MESH = pl.DeviceIdType.MESH
F32, BF16 = jnp.float32, jnp.bfloat16


def power_of_minus(e):
    value = jnp.ones(e.shape, F32)
    for bit in range(7):
        step = jnp.full(e.shape, 2.0 ** -(2**bit), F32)
        value = value * jnp.where(((e >> bit) & 1) == 1, step, 1.0)
    return value


def dot_nt(a, b):
    return lax.dot_general(a, b, (((1,), (1,)), ((), ())), preferred_element_type=F32)


def kernel(
    scale,
    codes_hbm, exps_hbm, cent_hbm, counters_hbm,
    sums_ref, mass_ref,
    codes, exps, cent, counters, pts, inv, tmp, logit, share, acc, massacc,
    stats, rm, y_out, y_in, y_sum, yz_out, yz_in, z_out, z_in, z_sum, zy_out, zy_in,
    m_out, my_in, mz_out, mz_in,
    load_sem, g_send, g_recv, s_send, s_recv, r_send, r_recv,
    y_send, y_recv, yz_send, yz_recv, z_send, z_recv, zy_send, zy_recv,
    my_send, my_recv, mz_send, mz_recv,
):
    p = lax.axis_index("pts")
    me = lax.axis_index("cells")
    x = lax.div(p, Y * ZH)
    y = lax.rem(lax.div(p, ZH), Y)
    zh = lax.rem(p, ZH)
    zl = lax.div(me, CORES)
    core = lax.rem(me, CORES)
    other = 1 - core
    peers = ZL * CORES
    half_chips = ZL // 2
    half = lax.div(zl, half_chips)
    rows, width = pts.shape[3:]
    line = ZL * CORES * rows
    lanes = line // 2
    slice_rows = cent.shape[1]
    z_rows = acc.shape[2]
    piece = width // (NY + NZ)

    def at_x(j):
        return ((lax.rem(x + j, X) * Y + y) * ZH + zh, me)

    def at_y(k):
        return ((x * Y + lax.rem(y + k, Y)) * ZH + zh, me)

    def at_z(k):
        return ((x * Y + y) * ZH + lax.rem(zh + k, ZH), me)

    def at_cells(k):
        return (p, lax.rem(me + k, peers))

    sibling = (p, zl * CORES + other)

    def send(src, dst, send_sem, recv_sem, device):
        return pltpu.make_async_remote_copy(
            src_ref=src, dst_ref=dst, send_sem=send_sem, recv_sem=recv_sem,
            device_id=device, device_id_type=MESH,
        )

    loads = [
        pltpu.make_async_copy(src, dst, load_sem.at[i])
        for i, (src, dst) in enumerate(
            ((exps_hbm, exps), (codes_hbm, codes), (counters_hbm, counters), (cent_hbm, cent))
        )
    ]
    for load in loads:
        load.start()

    barrier = pltpu.get_barrier_semaphore()

    def greet(device):
        pl.semaphore_signal(barrier, inc=1, device_id=device, device_id_type=MESH)

    for k in range(1, peers):
        greet(at_cells(k))
    for j in range(1, X):
        greet(at_x(j))
    for k in range(1, ZH):
        greet(at_z(k))
    for k in range(1, Y):
        greet(at_y(k))

    n_exp = exps.shape[1]
    diagonal = lax.broadcasted_iota(jnp.int32, (n_exp, n_exp), 0) == lax.broadcasted_iota(
        jnp.int32, (n_exp, n_exp), 1
    )
    loads[0].wait()
    powers = power_of_minus(exps[...])
    column = jnp.sum(jnp.where(diagonal, powers, 0.0), axis=1, keepdims=True)
    loads[1].wait()
    pts[x, zl, core] = (codes[...].astype(F32) * column).astype(BF16)

    pl.semaphore_wait(barrier, (Y - 1) + (ZH - 1) + (peers - 1) + (X - 1))

    def block(xx, zz, cc, device, sem):
        ref = pts.at[xx, zz, cc]
        return send(ref, ref, g_send.at[sem], g_recv.at[xx, zz, cc], device)

    for k in range(1, ZL):
        block(x, zl, core, (p, lax.rem(zl + k, ZL) * CORES + core), k).start()
    block(x, zl, core, sibling, 0).start()
    for j in range(1, X):
        block(x, zl, core, at_x(j), ZL - 1 + j).start()
    sem_zl = ZL + X - 1
    sem_x = sem_zl + (ZL - 1) * X

    square = (128, 128)
    eye = lax.broadcasted_iota(jnp.int32, square, 0) == lax.broadcasted_iota(jnp.int32, square, 1)
    loads[2].wait()

    def spread(g, carry):
        row = lax.rsqrt(counters[pl.ds(g, 1), :].astype(F32) + 1.0)
        col = jnp.sum(jnp.where(eye, row, 0.0), axis=1, keepdims=True)
        inv[pl.ds(pl.multiple_of(g * 128, 128), 128), :] = jnp.broadcast_to(col, square)
        return carry

    lax.fori_loop(0, counters.shape[0], spread, 0)
    loads[3].wait()

    def stat_copy(src, hh, k):
        ref = stats.at[src, hh]
        return send(ref, ref, s_send.at[k, hh], s_recv.at[src, hh], at_cells(k))

    def points_of(xx, hh):
        return pts[xx, pl.ds(hh * half_chips, half_chips)].reshape(lanes, width)

    def local_stats(hh):
        points = points_of(x, hh)

        def product(s, top):
            part = dot_nt(cent[s], points)
            tmp[s] = part
            return jnp.maximum(top, jnp.max(part, axis=0, keepdims=True))

        top = lax.fori_loop(0, X, product, jnp.full((1, lanes), -jnp.inf, F32))
        shift = top * scale

        def add_up(s, sums):
            expo = jnp.exp2(tmp[s] * scale - shift)
            weights = inv[pl.ds(pl.multiple_of(s * slice_rows, 128), slice_rows), :]
            weights = jnp.concatenate([weights] * (lanes // 128), axis=1)
            return (
                sums[0] + jnp.sum(expo, axis=0, keepdims=True),
                sums[1] + jnp.sum(expo * weights, axis=0, keepdims=True),
            )

        zero = jnp.zeros((1, lanes), F32)
        total, novel = lax.fori_loop(0, X, add_up, (zero, zero))
        stats[me, hh, 0:1, :] = top
        stats[me, hh, 1:2, :] = total
        stats[me, hh, 2:3, :] = novel

        def start(k, carry):
            stat_copy(me, hh, k).start()
            return carry

        lax.fori_loop(1, peers, start, 0)
        logit[x, :, pl.ds(pl.multiple_of(hh * lanes, 128), lanes)] = tmp[x]

    def forward(zz, slot):
        block(x, zz, core, sibling, 0).wait_recv()
        for j in range(1, X):
            block(x, zz, core, at_x(j), sem_zl + slot * X + j).start()
        block(x, zz, core, sibling, sem_zl + slot * X).start()

    begin = half * half_chips
    for k in range(1, half_chips):
        forward(begin + lax.rem(zl - begin + k, half_chips), k - 1)
    for k in range(half_chips):
        block(x, begin + k, other, sibling, 0).wait_recv()
    local_stats(half)
    begin = (1 - half) * half_chips
    for k in range(half_chips):
        forward(begin + k, half_chips - 1 + k)
    for k in range(half_chips):
        block(x, begin + k, other, sibling, 0).wait_recv()
    local_stats(1 - half)

    x_order = [1, 3, 2] if X == 4 else list(range(1, X))
    for i, j in enumerate(x_order):
        xx = lax.rem(x + j, X)

        def pass_on(zz, carry, i=i, xx=xx):
            block(xx, zz, core, sibling, 0).wait_recv()
            block(xx, zz, core, sibling, sem_x + i * ZL + zz).start()
            return carry

        lax.fori_loop(0, ZL, pass_on, 0)
    for j in x_order:
        xx = lax.rem(x + j, X)

        def arrived(zz, carry, xx=xx):
            block(xx, zz, other, sibling, 0).wait_recv()
            return carry

        lax.fori_loop(0, ZL, arrived, 0)
        logit[xx] = dot_nt(cent[x], pts[xx].reshape(line, width))

    def stats_in(k, carry):
        src = lax.rem(me + k, peers)
        for hh in range(2):
            stat_copy(src, hh, k).wait_recv()
        return carry

    lax.fori_loop(1, peers, stats_in, 0)
    for hh in range(2):
        here = slice(hh * lanes, (hh + 1) * lanes)
        tops = stats[:, hh, 0, :]
        top = jnp.max(tops, axis=0, keepdims=True)
        ratio = jnp.exp2((tops - top) * scale)
        total = jnp.sum(stats[:, hh, 1, :] * ratio, axis=0, keepdims=True)
        novel = jnp.sum(stats[:, hh, 2, :] * ratio, axis=0, keepdims=True)
        rm[x, 0:1, here] = top * scale
        rm[x, 1:2, here] = novel / total / total

    def rm_copy(src, j):
        return send(rm.at[src], rm.at[src], r_send.at[j], r_recv.at[src], at_x(j))

    for j in range(1, X):
        rm_copy(x, j).start()

    acc[...] = jnp.zeros(acc.shape, F32)
    massacc[...] = jnp.zeros(massacc.shape, F32)

    def accumulate(xx):
        for q in range(line // 128):
            here = slice(q * 128, (q + 1) * 128)
            shift, factor = rm[xx, 0:1, here], rm[xx, 1:2, here]
            part = (jnp.exp2(logit[xx, :, here] * scale - shift) * factor).astype(BF16)
            share[:, here] = part
            massacc[...] += part.astype(F32)
        acc[...] += jnp.dot(
            share[...], pts[xx].reshape(line, width), preferred_element_type=F32
        ).reshape(acc.shape)

    accumulate(x)
    for j in x_order:
        xx = lax.rem(x + j, X)
        rm_copy(xx, j).wait_recv()
        accumulate(xx)

    def y_copy(q, src, k, dst):
        return send(y_out.at[q, dst], y_in.at[q, src], y_send.at[q, k], y_recv.at[q, src], at_y(k))

    def z_copy(q, src, k, dst):
        return send(z_out.at[q, dst], z_in.at[q, src], z_send.at[q, k], z_recv.at[q, src], at_z(k))

    def yz_copy(q, src, k, dst):
        return send(
            yz_out.at[q, dst], yz_in.at[q, src], yz_send.at[q, k], yz_recv.at[q, src], at_z(k)
        )

    def zy_copy(q, src, k, dst):
        return send(
            zy_out.at[q, dst], zy_in.at[q, src], zy_send.at[q, k], zy_recv.at[q, src], at_y(k)
        )

    def my_copy(src, k):
        return send(m_out, my_in.at[src], my_send.at[k], my_recv.at[src], at_y(k))

    def mz_copy(src, k):
        return send(mz_out, mz_in.at[src], mz_send.at[k], mz_recv.at[src], at_z(k))

    def columns(q):
        return slice(q * piece, (q + 1) * piece)

    def over_y(step, first=0):
        return lax.fori_loop(1, Y, step, first)

    def over_z(step, first=0):
        return lax.fori_loop(1, ZH, step, first)

    def y_first(q):
        def start(k, carry):
            dst = lax.rem(y + k, Y)
            y_out[q, dst] = acc[dst, :, :, columns(q)].astype(BF16)
            y_copy(q, y, k, dst).start()
            return carry

        over_y(start)

    def z_first(q):
        def start(k, carry):
            dst = lax.rem(zh + k, ZH)
            z_out[q, dst] = acc[:, dst, :, columns(NY + q)].astype(BF16)
            z_copy(q, zh, k, dst).start()
            return carry

        over_z(start)

    def y_then_z(q):
        def add(k, total):
            src = lax.rem(y + k, Y)
            y_copy(q, src, k, src).wait_recv()
            return total + y_in[q, src].astype(F32)

        y_sum[q] = over_y(add, acc[y, :, :, columns(q)])

        def start(k, carry):
            dst = lax.rem(zh + k, ZH)
            yz_out[q, dst] = y_sum[q, dst].astype(BF16)
            yz_copy(q, zh, k, dst).start()
            return carry

        over_z(start)

    def z_then_y(q):
        def add(k, carry):
            src = lax.rem(zh + k, ZH)
            z_copy(q, src, k, src).wait_recv()
            z_sum[q] += z_in[q, src].astype(F32)
            return carry

        z_sum[q] = acc[:, zh, :, columns(NY + q)]
        over_z(add)

        def start(k, carry):
            dst = lax.rem(y + k, Y)
            zy_out[q, dst] = z_sum[q, dst].astype(BF16)
            zy_copy(q, y, k, dst).start()
            return carry

        over_y(start)

    def finish_y(q):
        def add(k, total):
            src = lax.rem(zh + k, ZH)
            yz_copy(q, src, k, src).wait_recv()
            return total + yz_in[q, src].astype(F32)

        sums_ref[:, columns(q)] = over_z(add, y_sum[q, zh])

    def finish_z(q):
        def add(k, total):
            src = lax.rem(y + k, Y)
            zy_copy(q, src, k, src).wait_recv()
            return total + zy_in[q, src].astype(F32)

        sums_ref[:, columns(NY + q)] = over_y(add, z_sum[q, y])

    for q in range(max(NY, NZ)):
        if q < NY:
            y_first(q)
        if q < NZ:
            z_first(q)

    m_out[...] = jnp.zeros(m_out.shape, F32)
    for g in range(slice_rows // 128):
        col = jnp.sum(massacc[g * 128 : (g + 1) * 128, :], axis=1, keepdims=True)
        m_out[g : g + 1, :] = jnp.sum(jnp.where(eye, col, 0.0), axis=0, keepdims=True)

    def my_start(k, carry):
        my_copy(y, k).start()
        return carry

    over_y(my_start)

    for q in range(max(NY, NZ)):
        if q < NY:
            y_then_z(q)
        if q < NZ:
            z_then_y(q)
        if q == 0:

            def my_add(k, total):
                src = lax.rem(y + k, Y)
                my_copy(src, k).wait_recv()
                return total + my_in[src]

            mass = over_y(my_add, m_out[...])
            mz_out[...] = mass

            def mz_start(k, carry):
                mz_copy(zh, k).start()
                return carry

            over_z(mz_start)

    def mz_add(k, total):
        src = lax.rem(zh + k, ZH)
        mz_copy(src, k).wait_recv()
        return total + mz_in[src]

    mass = over_z(mz_add, mass)
    per_row = 128 // z_rows
    place = y * ZH + zh
    at_line = lax.broadcasted_iota(jnp.int32, mass.shape, 0) == lax.div(place, per_row)
    picked = jnp.sum(jnp.where(at_line, mass, 0.0), axis=0, keepdims=True)
    which = lax.rem(place, per_row)
    answer = jnp.zeros((1, z_rows), F32)
    for q in range(per_row):
        answer = jnp.where(which == q, picked[:, q * z_rows : (q + 1) * z_rows], answer)
    mass_ref[...] = answer

    for q in range(max(NY, NZ)):
        if q < NY:
            finish_y(q)
        if q < NZ:
            finish_z(q)

    def sent_block(i, carry):
        block(x, zl, core, sibling, i).wait_send()
        return carry

    lax.fori_loop(0, g_send.shape[0], sent_block, 0)

    def sent_stats(k, carry):
        for hh in range(2):
            stat_copy(me, hh, k).wait_send()
        return carry

    lax.fori_loop(1, peers, sent_stats, 0)
    for j in range(1, X):
        rm_copy(x, j).wait_send()

    def sent_y(k, carry):
        dst = lax.rem(y + k, Y)
        for q in range(NY):
            y_copy(q, y, k, dst).wait_send()
        for q in range(NZ):
            zy_copy(q, y, k, dst).wait_send()
        my_copy(y, k).wait_send()
        return carry

    over_y(sent_y)

    def sent_z(k, carry):
        dst = lax.rem(zh + k, ZH)
        for q in range(NY):
            yz_copy(q, zh, k, dst).wait_send()
        for q in range(NZ):
            z_copy(q, zh, k, dst).wait_send()
        mz_copy(zh, k).wait_send()
        return carry

    over_z(sent_z)


def body(codes, exponents, centroids, counters):
    rows, width = codes.shape
    cells = centroids.shape[0]
    slice_rows = cells // X
    z_rows = slice_rows // Y // ZH
    line = ZL * CORES * rows
    lanes = line // 2
    peers = ZL * CORES
    piece = width // (NY + NZ)
    scale = 4.0 / math.sqrt(width) * math.log2(math.e)
    vmem, dma = pltpu.VMEM, pltpu.SemaphoreType.DMA
    hbm = pl.BlockSpec(memory_space=pltpu.HBM)
    sums, mass = pl.pallas_call(
        functools.partial(kernel, scale),
        out_shape=(
            jax.ShapeDtypeStruct((z_rows, width), F32),
            jax.ShapeDtypeStruct((1, z_rows), F32),
        ),
        in_specs=[hbm] * 4,
        out_specs=(pl.BlockSpec(memory_space=vmem), pl.BlockSpec(memory_space=vmem)),
        scratch_shapes=[
            vmem((rows, width), jnp.int32),
            vmem((1, rows), jnp.int32),
            vmem((X, slice_rows, width), BF16),
            vmem((cells // 128, 128), jnp.int32),
            vmem((X, ZL, CORES, rows, width), BF16),
            vmem((cells, 128), F32),
            vmem((X, slice_rows, lanes), F32),
            vmem((X, slice_rows, line), F32),
            vmem((slice_rows, line), BF16),
            vmem((Y, ZH, z_rows, width), F32),
            vmem((slice_rows, 128), F32),
            vmem((peers, 2, 8, lanes), F32),
            vmem((X, 8, line), F32),
            vmem((NY, Y, ZH, z_rows, piece), BF16),
            vmem((NY, Y, ZH, z_rows, piece), BF16),
            vmem((NY, ZH, z_rows, piece), F32),
            vmem((NY, ZH, z_rows, piece), BF16),
            vmem((NY, ZH, z_rows, piece), BF16),
            vmem((NZ, ZH, Y, z_rows, piece), BF16),
            vmem((NZ, ZH, Y, z_rows, piece), BF16),
            vmem((NZ, Y, z_rows, piece), F32),
            vmem((NZ, Y, z_rows, piece), BF16),
            vmem((NZ, Y, z_rows, piece), BF16),
            vmem((8, 128), F32),
            vmem((Y, 8, 128), F32),
            vmem((8, 128), F32),
            vmem((ZH, 8, 128), F32),
            dma((4,)),
            dma((X + ZL - 1 + (ZL - 1) * X + (X - 1) * ZL,)),
            dma((X, ZL, CORES)),
            dma((peers, 2)),
            dma((peers, 2)),
            dma((X,)),
            dma((X,)),
            dma((NY, Y)),
            dma((NY, Y)),
            dma((NY, ZH)),
            dma((NY, ZH)),
            dma((NZ, ZH)),
            dma((NZ, ZH)),
            dma((NZ, Y)),
            dma((NZ, Y)),
            dma((Y,)),
            dma((Y,)),
            dma((ZH,)),
            dma((ZH,)),
        ],
        compiler_params=pltpu.CompilerParams(
            collective_id=0, has_side_effects=True, vmem_limit_bytes=56 << 20
        ),
    )(
        codes,
        exponents.reshape(1, rows),
        centroids.reshape(X, slice_rows, width),
        counters.reshape(cells // 128, 128),
    )
    return sums[None], mass


def solution(mesh):
    in_specs = (P(("pts", "cells"), None), P(("pts", "cells")), P("cells", None), P("cells"))
    out_specs = (P("cells", "pts", None), P("cells", "pts"))
    return jax.shard_map(body, mesh=mesh, in_specs=in_specs, out_specs=out_specs, check_vma=False)
```

time: 78 us -> 65.8 us (0.84)
  Pallas kernels: 70.9 us -> 62.1 us
  local copies, waits for them, and re-layouts: 5.29 us -> 2.59 us
    pallas_call x1, Pallas kernels: 70.9 us -> 62.1 us  [body(): pl.pallas_call(functools.partial(kernel, scale), out_shape=(jax.ShapeDtyp...]
    unnamed x10 -> x2, local copies, waits for them, and re-layouts: 5.29 us -> 2.59 us
where the time goes in v2:
time: 65.8 us; the launch traced here: 65.3 us
  Pallas kernels  62.1 us (94%)
  local copies, waits for them, and re-layouts  2.59 us (4%)
    pallas_call x1, Pallas kernels, body(): pl.pallas_call(functools.partial(kernel, scale), out_shape=(jax.ShapeDtyp...  62.1 us
    unnamed x2, local copies, waits for them, and re-layouts  2.59 us

profile of v2, /device:TPU:1, one launch (start us, length us, event | category | flops | bytes accessed | tf_op | source)
XLA Modules:
  0.0 65.3 jit_solution(5901279385782389657)
XLA Ops:
  0.6 62.1 %shard_map.59 = (f32[32,512]{1,0:T(8,128)}, f32[1,32]{1,0:T(1,128)}) custom-call(s32[64,512]{1,0:T(8,128)} %codes_hbm.1, s32[1,64]{1,0:T(1,128)} %bitcast.7, bf16[4,768,512]{2,1,0:T(8,128)(2,1)} %bitcast.4, s32[24,128]{1,0:T(8,128)} %bitcast.6), custom_call_target="tpu_custom_call" | custom-call | tf_op jit(solution)/shard_map/pallas_call | solution.py:469
  62.8 1.5 %copy.8 = f32[1,32,512]{2,1,0:T(8,128)} copy(f32[1,32,512]{2,1,0:T(8,128)} %bitcast.5) | data formatting | bytes 131072
  64.2 1.1 %copy.9 = f32[1,32]{1,0:T(1,128)} copy(f32[1,32]{1,0:T(1,128)} %get-tuple-element.9) | data formatting | bytes 256

commit v3 on v2

--- a/solution.py
+++ b/solution.py
@@ -9,7 +9,10 @@
 from jax.sharding import PartitionSpec as P
 
 X, Y, ZH, ZL, CORES = 4, 8, 3, 4, 2
-NY, NZ = 2, 2
+HALVES, QUARTERS = 2, 4
+Y_PIECES = (((0, 2), (0, 1)), ((0, 2), (1, 2)), ((0, 1), (2, 3)))
+Z_PIECES = (((0, 2), (3, 4)), ((1, 2), (2, 3)))
+NY, NZ = len(Y_PIECES), len(Z_PIECES)
 MESH = pl.DeviceIdType.MESH
 F32, BF16 = jnp.float32, jnp.bfloat16
 
@@ -53,7 +56,14 @@
     lanes = line // 2
     slice_rows = cent.shape[1]
     z_rows = acc.shape[2]
-    piece = width // (NY + NZ)
+
+    def cut(piece):
+        high, wide = z_rows // HALVES, width // QUARTERS
+        (r0, r1), (c0, c1) = piece
+        return slice(r0 * high, r1 * high), slice(c0 * wide, c1 * wide)
+
+    y_cuts = [cut(piece) for piece in Y_PIECES]
+    z_cuts = [cut(piece) for piece in Z_PIECES]
 
     def at_x(j):
         return ((lax.rem(x + j, X) * Y + y) * ZH + zh, me)
@@ -195,24 +205,22 @@
     local_stats(1 - half)
 
     x_order = [1, 3, 2] if X == 4 else list(range(1, X))
-    for i, j in enumerate(x_order):
+
+    def pass_on(hh):
+        for i, j in enumerate(x_order):
+            xx = lax.rem(x + j, X)
+            for k in range(half_chips):
+                zz = hh * half_chips + k
+                block(xx, zz, core, sibling, 0).wait_recv()
+                block(xx, zz, core, sibling, sem_x + i * ZL + zz).start()
+
+    def x_logits(j):
         xx = lax.rem(x + j, X)
-
-        def pass_on(zz, carry, i=i, xx=xx):
-            block(xx, zz, core, sibling, 0).wait_recv()
-            block(xx, zz, core, sibling, sem_x + i * ZL + zz).start()
-            return carry
-
-        lax.fori_loop(0, ZL, pass_on, 0)
-    for j in x_order:
-        xx = lax.rem(x + j, X)
-
-        def arrived(zz, carry, xx=xx):
+        for zz in range(ZL):
             block(xx, zz, other, sibling, 0).wait_recv()
-            return carry
-
-        lax.fori_loop(0, ZL, arrived, 0)
         logit[xx] = dot_nt(cent[x], pts[xx].reshape(line, width))
+
+    pass_on(half)
 
     def stats_in(k, carry):
         src = lax.rem(me + k, peers)
@@ -251,26 +259,29 @@
             share[...], pts[xx].reshape(line, width), preferred_element_type=F32
         ).reshape(acc.shape)
 
+    pass_on(1 - half)
     accumulate(x)
+    for j in x_order:
+        x_logits(j)
     for j in x_order:
         xx = lax.rem(x + j, X)
         rm_copy(xx, j).wait_recv()
         accumulate(xx)
 
     def y_copy(q, src, k, dst):
-        return send(y_out.at[q, dst], y_in.at[q, src], y_send.at[q, k], y_recv.at[q, src], at_y(k))
+        return send(y_out[q].at[dst], y_in[q].at[src], y_send.at[q, k], y_recv.at[q, src], at_y(k))
 
     def z_copy(q, src, k, dst):
-        return send(z_out.at[q, dst], z_in.at[q, src], z_send.at[q, k], z_recv.at[q, src], at_z(k))
+        return send(z_out[q].at[dst], z_in[q].at[src], z_send.at[q, k], z_recv.at[q, src], at_z(k))
 
     def yz_copy(q, src, k, dst):
         return send(
-            yz_out.at[q, dst], yz_in.at[q, src], yz_send.at[q, k], yz_recv.at[q, src], at_z(k)
+            yz_out[q].at[dst], yz_in[q].at[src], yz_send.at[q, k], yz_recv.at[q, src], at_z(k)
         )
 
     def zy_copy(q, src, k, dst):
         return send(
-            zy_out.at[q, dst], zy_in.at[q, src], zy_send.at[q, k], zy_recv.at[q, src], at_y(k)
+            zy_out[q].at[dst], zy_in[q].at[src], zy_send.at[q, k], zy_recv.at[q, src], at_y(k)
         )
 
     def my_copy(src, k):
@@ -278,9 +289,6 @@
 
     def mz_copy(src, k):
         return send(mz_out, mz_in.at[src], mz_send.at[k], mz_recv.at[src], at_z(k))
-
-    def columns(q):
-        return slice(q * piece, (q + 1) * piece)
 
     def over_y(step, first=0):
         return lax.fori_loop(1, Y, step, first)
@@ -291,7 +299,7 @@
     def y_first(q):
         def start(k, carry):
             dst = lax.rem(y + k, Y)
-            y_out[q, dst] = acc[dst, :, :, columns(q)].astype(BF16)
+            y_out[q][dst] = acc[dst, :, *y_cuts[q]].astype(BF16)
             y_copy(q, y, k, dst).start()
             return carry
 
@@ -300,7 +308,7 @@
     def z_first(q):
         def start(k, carry):
             dst = lax.rem(zh + k, ZH)
-            z_out[q, dst] = acc[:, dst, :, columns(NY + q)].astype(BF16)
+            z_out[q][dst] = acc[:, dst, *z_cuts[q]].astype(BF16)
             z_copy(q, zh, k, dst).start()
             return carry
 
@@ -310,13 +318,13 @@
         def add(k, total):
             src = lax.rem(y + k, Y)
             y_copy(q, src, k, src).wait_recv()
-            return total + y_in[q, src].astype(F32)
-
-        y_sum[q] = over_y(add, acc[y, :, :, columns(q)])
+            return total + y_in[q][src].astype(F32)
+
+        y_sum[q][...] = over_y(add, acc[y, :, *y_cuts[q]])
 
         def start(k, carry):
             dst = lax.rem(zh + k, ZH)
-            yz_out[q, dst] = y_sum[q, dst].astype(BF16)
+            yz_out[q][dst] = y_sum[q][dst].astype(BF16)
             yz_copy(q, zh, k, dst).start()
             return carry
 
@@ -326,15 +334,15 @@
         def add(k, carry):
             src = lax.rem(zh + k, ZH)
             z_copy(q, src, k, src).wait_recv()
-            z_sum[q] += z_in[q, src].astype(F32)
+            z_sum[q][...] += z_in[q][src].astype(F32)
             return carry
 
-        z_sum[q] = acc[:, zh, :, columns(NY + q)]
+        z_sum[q][...] = acc[:, zh, *z_cuts[q]]
         over_z(add)
 
         def start(k, carry):
             dst = lax.rem(y + k, Y)
-            zy_out[q, dst] = z_sum[q, dst].astype(BF16)
+            zy_out[q][dst] = z_sum[q][dst].astype(BF16)
             zy_copy(q, y, k, dst).start()
             return carry
 
@@ -344,17 +352,17 @@
         def add(k, total):
             src = lax.rem(zh + k, ZH)
             yz_copy(q, src, k, src).wait_recv()
-            return total + yz_in[q, src].astype(F32)
-
-        sums_ref[:, columns(q)] = over_z(add, y_sum[q, zh])
+            return total + yz_in[q][src].astype(F32)
+
+        sums_ref[*y_cuts[q]] = over_z(add, y_sum[q][zh])
 
     def finish_z(q):
         def add(k, total):
             src = lax.rem(y + k, Y)
             zy_copy(q, src, k, src).wait_recv()
-            return total + zy_in[q, src].astype(F32)
-
-        sums_ref[:, columns(NY + q)] = over_y(add, z_sum[q, y])
+            return total + zy_in[q][src].astype(F32)
+
+        sums_ref[*z_cuts[q]] = over_y(add, z_sum[q][y])
 
     for q in range(max(NY, NZ)):
         if q < NY:
@@ -462,7 +470,13 @@
     line = ZL * CORES * rows
     lanes = line // 2
     peers = ZL * CORES
-    piece = width // (NY + NZ)
+
+    def size(piece):
+        (r0, r1), (c0, c1) = piece
+        return (r1 - r0) * z_rows // HALVES, (c1 - c0) * width // QUARTERS
+
+    y_sizes = [size(piece) for piece in Y_PIECES]
+    z_sizes = [size(piece) for piece in Z_PIECES]
     scale = 4.0 / math.sqrt(width) * math.log2(math.e)
     vmem, dma = pltpu.VMEM, pltpu.SemaphoreType.DMA
     hbm = pl.BlockSpec(memory_space=pltpu.HBM)
@@ -488,16 +502,16 @@
             vmem((slice_rows, 128), F32),
             vmem((peers, 2, 8, lanes), F32),
             vmem((X, 8, line), F32),
-            vmem((NY, Y, ZH, z_rows, piece), BF16),
-            vmem((NY, Y, ZH, z_rows, piece), BF16),
-            vmem((NY, ZH, z_rows, piece), F32),
-            vmem((NY, ZH, z_rows, piece), BF16),
-            vmem((NY, ZH, z_rows, piece), BF16),
-            vmem((NZ, ZH, Y, z_rows, piece), BF16),
-            vmem((NZ, ZH, Y, z_rows, piece), BF16),
-            vmem((NZ, Y, z_rows, piece), F32),
-            vmem((NZ, Y, z_rows, piece), BF16),
-            vmem((NZ, Y, z_rows, piece), BF16),
+            [vmem((Y, ZH, *size), BF16) for size in y_sizes],
+            [vmem((Y, ZH, *size), BF16) for size in y_sizes],
+            [vmem((ZH, *size), F32) for size in y_sizes],
+            [vmem((ZH, *size), BF16) for size in y_sizes],
+            [vmem((ZH, *size), BF16) for size in y_sizes],
+            [vmem((ZH, Y, *size), BF16) for size in z_sizes],
+            [vmem((ZH, Y, *size), BF16) for size in z_sizes],
+            [vmem((Y, *size), F32) for size in z_sizes],
+            [vmem((Y, *size), BF16) for size in z_sizes],
+            [vmem((Y, *size), BF16) for size in z_sizes],
             vmem((8, 128), F32),
             vmem((Y, 8, 128), F32),
             vmem((8, 128), F32),
@@ -523,14 +537,17 @@
             dma((ZH,)),
         ],
         compiler_params=pltpu.CompilerParams(
-            collective_id=0, has_side_effects=True, vmem_limit_bytes=56 << 20
+            collective_id=0, has_side_effects=True, vmem_limit_bytes=48 << 20
         ),
-    )(
-        codes,
-        exponents.reshape(1, rows),
-        centroids.reshape(X, slice_rows, width),
-        counters.reshape(cells // 128, 128),
-    )
+    )(*(
+        pltpu.with_memory_space_constraint(a, pltpu.HBM)
+        for a in (
+            codes,
+            exponents.reshape(1, rows),
+            centroids.reshape(X, slice_rows, width),
+            counters.reshape(cells // 128, 128),
+        )
+    ))
     return sums[None], mass
 
 

time: 65.8 us -> 64.1 us (0.974)
  local copies, waits for them, and re-layouts: 2.59 us -> 1.14 us
    unnamed x2, local copies, waits for them, and re-layouts: 2.59 us -> 1.14 us
where the time goes in v3:
time: 64.1 us; the launch traced here: 63.9 us
  Pallas kernels  62.1 us (97%)
  local copies, waits for them, and re-layouts  1.14 us (2%)
    pallas_call x1, Pallas kernels, body(): pl.pallas_call(functools.partial(kernel, scale), out_shape=(jax.ShapeDtyp...  62.1 us

profile of v3, /device:TPU:1, one launch (start us, length us, event | category | flops | bytes accessed | tf_op | source)
XLA Modules:
  0.0 63.9 jit_solution(1039881351989818483)
XLA Ops:
  0.6 62.1 %shard_map.59 = (f32[32,512]{1,0:T(8,128)S(1)}, f32[1,32]{1,0:T(1,128)S(1)}) custom-call(s32[64,512]{1,0:T(8,128)} %codes_hbm.1, s32[1,64]{1,0:T(1,128)} %bitcast.7, bf16[4,768,512]{2,1,0:T(8,128)(2,1)} %bitcast.5, s32[24,128]{1,0:T(8,128)} %bitcast.6), custom_call_target="tpu_custom_call" | custom-call | tf_op jit(solution)/shard_map/pallas_call | solution.py:483
  62.7 0.6 copy.8
  63.4 0.5 copy.9

commit v4 on v3

--- a/solution.py
+++ b/solution.py
@@ -10,7 +10,7 @@
 
 X, Y, ZH, ZL, CORES = 4, 8, 3, 4, 2
 HALVES, QUARTERS = 2, 4
-Y_PIECES = (((0, 2), (0, 1)), ((0, 2), (1, 2)), ((0, 1), (2, 3)))
+Y_PIECES = (((0, 2), (0, 2)), ((0, 1), (2, 3)))
 Z_PIECES = (((0, 2), (3, 4)), ((1, 2), (2, 3)))
 NY, NZ = len(Y_PIECES), len(Z_PIECES)
 MESH = pl.DeviceIdType.MESH
@@ -91,7 +91,7 @@
             ((exps_hbm, exps), (codes_hbm, codes), (counters_hbm, counters), (cent_hbm, cent))
         )
     ]
-    for load in loads:
+    for load in loads[:2]:
         load.start()
 
     barrier = pltpu.get_barrier_semaphore()
@@ -99,14 +99,17 @@
     def greet(device):
         pl.semaphore_signal(barrier, inc=1, device_id=device, device_id_type=MESH)
 
+    for k in sorted(range(1, Y), key=lambda k: -min(k, Y - k)):
+        greet(at_y(k))
+    for k in range(1, ZH):
+        greet(at_z(k))
     for k in range(1, peers):
         greet(at_cells(k))
     for j in range(1, X):
         greet(at_x(j))
-    for k in range(1, ZH):
-        greet(at_z(k))
-    for k in range(1, Y):
-        greet(at_y(k))
+
+    for load in loads[2:]:
+        load.start()
 
     n_exp = exps.shape[1]
     diagonal = lax.broadcasted_iota(jnp.int32, (n_exp, n_exp), 0) == lax.broadcasted_iota(
@@ -187,9 +190,9 @@
 
     def forward(zz, slot):
         block(x, zz, core, sibling, 0).wait_recv()
+        block(x, zz, core, sibling, sem_zl + slot * X).start()
         for j in range(1, X):
             block(x, zz, core, at_x(j), sem_zl + slot * X + j).start()
-        block(x, zz, core, sibling, sem_zl + slot * X).start()
 
     begin = half * half_chips
     for k in range(1, half_chips):
@@ -248,25 +251,31 @@
     acc[...] = jnp.zeros(acc.shape, F32)
     massacc[...] = jnp.zeros(massacc.shape, F32)
 
-    def accumulate(xx):
+    def weigh(xx, slot):
         for q in range(line // 128):
             here = slice(q * 128, (q + 1) * 128)
             shift, factor = rm[xx, 0:1, here], rm[xx, 1:2, here]
             part = (jnp.exp2(logit[xx, :, here] * scale - shift) * factor).astype(BF16)
-            share[:, here] = part
+            share[slot][:, here] = part
             massacc[...] += part.astype(F32)
+
+    def add_product(xx, slot):
         acc[...] += jnp.dot(
-            share[...], pts[xx].reshape(line, width), preferred_element_type=F32
+            share[slot][...], pts[xx].reshape(line, width), preferred_element_type=F32
         ).reshape(acc.shape)
 
     pass_on(1 - half)
-    accumulate(x)
+    weigh(x, 0)
+    add_product(x, 0)
     for j in x_order:
         x_logits(j)
     for j in x_order:
-        xx = lax.rem(x + j, X)
-        rm_copy(xx, j).wait_recv()
-        accumulate(xx)
+        rm_copy(lax.rem(x + j, X), j).wait_recv()
+    for i, j in enumerate(x_order):
+        weigh(lax.rem(x + j, X), i)
+        if i > 0:
+            add_product(lax.rem(x + x_order[i - 1], X), i - 1)
+    add_product(lax.rem(x + x_order[-1], X), len(x_order) - 1)
 
     def y_copy(q, src, k, dst):
         return send(y_out[q].at[dst], y_in[q].at[src], y_send.at[q, k], y_recv.at[q, src], at_y(k))
@@ -365,10 +374,10 @@
         sums_ref[*z_cuts[q]] = over_y(add, z_sum[q][y])
 
     for q in range(max(NY, NZ)):
+        if q < NZ:
+            z_first(q)
         if q < NY:
             y_first(q)
-        if q < NZ:
-            z_first(q)
 
     m_out[...] = jnp.zeros(m_out.shape, F32)
     for g in range(slice_rows // 128):
@@ -497,11 +506,11 @@
             vmem((cells, 128), F32),
             vmem((X, slice_rows, lanes), F32),
             vmem((X, slice_rows, line), F32),
-            vmem((slice_rows, line), BF16),
+            [vmem((slice_rows, line), BF16) for _ in range(X - 1)],
             vmem((Y, ZH, z_rows, width), F32),
             vmem((slice_rows, 128), F32),
-            vmem((peers, 2, 8, lanes), F32),
-            vmem((X, 8, line), F32),
+            vmem((peers, 2, 4, lanes), F32),
+            vmem((X, 2, line), F32),
             [vmem((Y, ZH, *size), BF16) for size in y_sizes],
             [vmem((Y, ZH, *size), BF16) for size in y_sizes],
             [vmem((ZH, *size), F32) for size in y_sizes],

time: 64.1 us -> 64 us (level)
  no operation moved by 1% of the time
where the time goes in v4:
time: 64 us; the launch traced here: 63.9 us
  Pallas kernels  62.1 us (97%)
  local copies, waits for them, and re-layouts  1.14 us (2%)
  between operations  0.64 us (1%)
    pallas_call x1, Pallas kernels, body(): pl.pallas_call(functools.partial(kernel, scale), out_shape=(jax.ShapeDtyp...  62.1 us

profile of v4, /device:TPU:1, one launch (start us, length us, event | category | flops | bytes accessed | tf_op | source)
XLA Modules:
  0.0 63.9 jit_solution(14928904265469718207)
XLA Ops:
  0.6 62.1 %shard_map.59 = (f32[32,512]{1,0:T(8,128)S(1)}, f32[1,32]{1,0:T(1,128)S(1)}) custom-call(s32[64,512]{1,0:T(8,128)} %codes_hbm.1, s32[1,64]{1,0:T(1,128)} %bitcast.7, bf16[4,768,512]{2,1,0:T(8,128)(2,1)} %bitcast.5, s32[24,128]{1,0:T(8,128)} %bitcast.6), custom_call_target="tpu_custom_call" | custom-call | tf_op jit(solution)/shard_map/pallas_call | solution.py:492
  62.7 0.6 copy.8
  63.4 0.5 copy.9

commit v5 on v4

--- a/solution.py
+++ b/solution.py
@@ -391,10 +391,11 @@
     over_y(my_start)
 
     for q in range(max(NY, NZ)):
+        if q == 0:
+            for r in range(NZ):
+                z_then_y(r)
         if q < NY:
             y_then_z(q)
-        if q < NZ:
-            z_then_y(q)
         if q == 0:
 
             def my_add(k, total):

time: 64 us -> 64 us (level)
  no operation moved by 1% of the time
where the time goes in v5:
time: 64 us; the launch traced here: 63.8 us
  Pallas kernels  62.1 us (97%)
  local copies, waits for them, and re-layouts  1.14 us (2%)
  between operations  0.64 us (1%)
    pallas_call x1, Pallas kernels, body(): pl.pallas_call(functools.partial(kernel, scale), out_shape=(jax.ShapeDtyp...  62.1 us

profile of v5, /device:TPU:1, one launch (start us, length us, event | category | flops | bytes accessed | tf_op | source)
XLA Modules:
  0.0 63.8 jit_solution(14133560153497511954)
XLA Ops:
  0.6 62.1 %shard_map.59 = (f32[32,512]{1,0:T(8,128)S(1)}, f32[1,32]{1,0:T(1,128)S(1)}) custom-call(s32[64,512]{1,0:T(8,128)} %codes_hbm.1, s32[1,64]{1,0:T(1,128)} %bitcast.7, bf16[4,768,512]{2,1,0:T(8,128)(2,1)} %bitcast.5, s32[24,128]{1,0:T(8,128)} %bitcast.6), custom_call_target="tpu_custom_call" | custom-call | tf_op jit(solution)/shard_map/pallas_call | solution.py:493
  62.7 0.6 copy.8
  63.3 0.5 copy.9
